TPU v7x, 512 devices: a whole 4x8x8 slice. The times are simulated.
512 devices in a mesh: dp: 32 (over x, y), region: 16 (over z, core).
Axes of the slice: x: 4, y: 8, z: 8, core: 2. Of those that a mesh axis runs over, the one named last changes fastest.
Arguments:
- inputs: bfloat16 [32, 2, 4096, 256], P('dp', None, 'region'), may hold values from -6 to 6
- cotangent: bfloat16 [32, 2, 4096, 256], P('dp', None, 'region'), may hold values from -6 to 6
- w_filter: bfloat16 [2, 256, 256], replicated, may hold values from -0.25 to 0.25
- w_gate: bfloat16 [2, 256, 256], replicated, may hold values from -0.25 to 0.25
- w_mix: bfloat16 [2, 256, 256], replicated, may hold values from -0.25 to 0.25
- neighbours: int32 [32, 6], replicated, may hold values from 0 to 31, as said below
- adjacency: bfloat16 [32, 6, 128, 128], P('region'), may hold values from -0.21875 to 0.21875
Outputs:
- grad_inputs: bfloat16 [32, 2, 4096, 256], P('dp', None, 'region')
- grad_filter: float32 [2, 256, 256], replicated
- grad_gate: float32 [2, 256, 256], replicated
- grad_mix: float32 [2, 256, 256], replicated
Inputs may be any that keep to these rules, and one draw needn't show every extreme that they name: `neighbours`: for every region r (tiles r * 2 to (r + 1) * 2 - 1), exactly 11 of the 12 entries of its tiles' lists name tiles of other regions, each of a different region, so at most 1 name tiles of any one other region; all other entries name tiles of region r.
All inputs are finite; a program needn't handle non-finite values.
Results may differ from a plain program's by a relative error of at most 0.0053.
Values may be sent and summed in bfloat16 or wider, within the bound.
A program may use at most 64 MiB of HBM per device.

v0:
```python
import math
import jax
import jax.numpy as jnp
from jax import lax
from jax.sharding import PartitionSpec as P

CAP = 1


def per_device(inputs, cotangent, w_filter, w_gate, w_mix, neighbours, adjacency):
    regions = lax.axis_size("region")
    region_id = lax.axis_index("region")
    windows, steps, site_count, chans = inputs.shape
    tiles_dev = site_count // 128
    per_tile = neighbours.shape[1]
    entries = tiles_dev * per_tile
    capacity = CAP
    table = neighbours.reshape(regions, entries)
    owners = table // tiles_dev
    local_tile = table % tiles_dev
    sources = jnp.arange(regions, dtype=jnp.int32)
    positions = jnp.arange(entries)
    earlier = positions[:, None] > positions[None, :]
    ranks = jnp.sum(
        ((owners[:, :, None] == owners[:, None, :]) & earlier[None]).astype(jnp.int32), axis=2
    )
    slot_ids = jnp.arange(capacity)
    remote_entry = owners != sources[:, None]
    hits = (
        (owners[:, None, :] == region_id)
        & (ranks[:, None, :] == slot_ids[None, :, None])
        & remote_entry[:, None, :]
    )
    send_tile = jnp.sum(jnp.where(hits, local_tile[:, None, :], 0), axis=2).reshape(-1)
    send_used = jnp.any(hits, axis=2).reshape(-1)
    own_owner = lax.dynamic_index_in_dim(owners, region_id, 0, keepdims=False)
    own_rank = lax.dynamic_index_in_dim(ranks, region_id, 0, keepdims=False)
    own_tiles = lax.dynamic_index_in_dim(table, region_id, 0, keepdims=False)
    own_local_tile = lax.dynamic_index_in_dim(local_tile, region_id, 0, keepdims=False)
    at_home = own_owner == region_id
    drop_index = jnp.where(at_home, regions * capacity, own_owner * capacity + own_rank)
    w_cat = jnp.concatenate(
        [
            jnp.concatenate([w_filter[0], w_gate[0]], axis=1),
            jnp.concatenate([w_filter[1], w_gate[1]], axis=1),
        ],
        axis=0,
    )
    w_mixed = w_mix.reshape(2 * chans, chans)
    previous = jnp.concatenate([jnp.zeros_like(inputs[:, :1]), inputs[:, :-1]], axis=1)
    joint = jnp.concatenate([inputs, previous], axis=3)
    act = jnp.einsum("btsi,io->btso", joint, w_cat, preferred_element_type=jnp.float32)
    filt = jnp.tanh(act[..., :chans])
    gate = jax.nn.sigmoid(act[..., chans:])
    hidden = (filt * gate).astype(jnp.bfloat16)
    tiled = hidden.reshape(windows, steps, tiles_dev, 128, chans)
    piece = lax.all_gather(tiled, "region", axis=2, tiled=True)
    count = piece.shape[2]
    select = (own_tiles[:, None] == jnp.arange(count)[None, :]).astype(jnp.bfloat16)
    chosen = jnp.einsum("en,btnqc->bteqc", select, piece, preferred_element_type=jnp.float32)
    chosen = chosen.astype(jnp.bfloat16).reshape(windows, steps, tiles_dev, per_tile, 128, chans)
    graph_sum = jnp.einsum(
        "jkpq,btjkqc->btjpc", adjacency, chosen, preferred_element_type=jnp.float32
    )
    graph = graph_sum.astype(jnp.bfloat16).reshape(windows, steps, site_count, chans)
    both = jnp.concatenate([hidden, graph], axis=3)
    mix_sum = jnp.einsum("btsi,btsc->ic", both, cotangent, preferred_element_type=jnp.float32)
    back = jnp.einsum("btsc,ic->btsi", cotangent, w_mixed, preferred_element_type=jnp.float32)
    direct = back[..., :chans]
    graph_cot = (
        back[..., chans:].astype(jnp.bfloat16).reshape(windows, steps, tiles_dev, 128, chans)
    )
    term = jnp.einsum(
        "jkpq,btjpc->btjkqc", adjacency, graph_cot, preferred_element_type=jnp.float32
    )
    term = term.astype(jnp.bfloat16).reshape(windows, steps, entries, 128, chans)
    outgoing_back = jnp.zeros((windows, steps, regions * capacity, 128, chans), jnp.bfloat16)
    outgoing_back = outgoing_back.at[:, :, drop_index].set(term, mode="drop")
    outgoing_back = outgoing_back.reshape(windows, steps, regions, capacity, 128, chans)
    returned = lax.all_to_all(outgoing_back, "region", split_axis=2, concat_axis=2, tiled=True)
    returned = returned.reshape(windows, steps, regions * capacity, 128, chans)
    owner_hot = (
        (send_tile[None, :] == jnp.arange(tiles_dev)[:, None]) & send_used[None, :]
    ).astype(jnp.bfloat16)
    graph_grad = jnp.einsum(
        "ln,btnqc->btlqc", owner_hot, returned, preferred_element_type=jnp.float32
    )
    home_hot = (
        (own_local_tile[None, :] == jnp.arange(tiles_dev)[:, None]) & at_home[None, :]
    ).astype(jnp.bfloat16)
    home_grad = jnp.einsum("le,bteqc->btlqc", home_hot, term, preferred_element_type=jnp.float32)
    grad_hidden = direct + (graph_grad + home_grad).reshape(windows, steps, site_count, chans)
    act_cot = jnp.concatenate(
        [grad_hidden * gate * (1.0 - filt * filt), grad_hidden * filt * gate * (1.0 - gate)], axis=3
    ).astype(jnp.bfloat16)
    conv_sum = jnp.einsum("btsi,btso->io", joint, act_cot, preferred_element_type=jnp.float32)
    back_in = jnp.einsum("btso,io->btsi", act_cot, w_cat, preferred_element_type=jnp.float32)
    later = jnp.concatenate(
        [back_in[:, 1:, :, chans:], jnp.zeros((windows, 1, site_count, chans), jnp.float32)], axis=1
    )
    grad_inputs = (cotangent.astype(jnp.float32) + back_in[..., :chans] + later).astype(
        jnp.bfloat16
    )
    conv_total, mix_total = lax.psum((conv_sum, mix_sum), ("dp", "region"))
    total_rows = windows * lax.axis_size("dp") * steps * site_count * regions
    factor = 1.0 / math.sqrt(total_rows)
    grad_filter = (conv_total[:, :chans] * factor).reshape(2, chans, chans)
    grad_gate = (conv_total[:, chans:] * factor).reshape(2, chans, chans)
    grad_mix = (mix_total * factor).reshape(2, chans, chans)
    return (grad_inputs, grad_filter, grad_gate, grad_mix)


def solution(mesh):
    return jax.shard_map(
        per_device,
        mesh=mesh,
        in_specs=(
            P("dp", None, "region", None),
            P("dp", None, "region", None),
            P(),
            P(),
            P(),
            P(),
            P("region", None, None, None),
        ),
        out_specs=(P("dp", None, "region", None), P(), P(), P()),
        check_vma=False,
    )
```

profile of v0, /device:TPU:17, one launch (start us, length us, event | category | flops | bytes accessed | tf_op | source)
XLA Modules:
  0.0 429.3 jit_solution(3742528526093285278)
XLA Ops:
  7.2 0.0 copy-start
  7.2 0.8 copy.73
  8.0 0.1 reshape.354
  8.1 0.6 copy-done.15
  8.7 0.1 copy.74
  8.8 0.6 negate_select_fusion.4
  9.4 0.1 copy.78
  9.5 0.8 fusion.81
  10.2 0.4 convert_reduce_fusion
  10.6 0.0 copy-start.11
  10.6 0.2 select_reduce_fusion
  10.8 0.6 fusion.70
  11.4 1.4 convolution_bitcast_fusion
  12.7 0.0 copy-start.1
  12.8 0.9 copy-done.1
  13.7 0.0 copy-done.9
  13.7 0.0 copy-done.11
  13.7 0.0 copy-done
  13.7 0.6 fusion.12
  14.3 0.7 copy.80
  15.0 0.1 copy.81
  15.2 1.6 broadcast.246
  16.8 5.3 %scatter_fusion = bf16[2,16,128,256]{3,2,1,0:T(8,128)(2,1)} fusion(bf16[2,16,128,256]{3,2,1,0:T(8,128)(2,1)} %broadcast.246, s32[12]{0:T(128)} %fusion.70, bf16[12,2,128,256]{3,2,1,0:T(8,128)(2,1)S(1)} %copy.81), kind=kCustom, calls=%fused_computation | custom fusion | bytes 4718640 | tf_op jit(solution)/shard_map/scatter | solution.py:78
  22.0 3.1 copy.82
  25.2 0.0 copy-start.5
  25.2 0.0 copy-start.6
  25.2 11.1 %all-to-all-start = ((bf16[1,2,16,1,128,256]{5,4,1,3,0,2:T(8,128)(2,1)}), bf16[1,2,16,1,128,256]{5,4,1,3,0,2:T(8,128)(2,1)}, u32[]{:S(2)}, u32[]{:S(2)}) async-start(bf16[1,2,16,1,128,256]{5,4,1,3,0,2:T(8,128)(2,1)} %copy.82), calls=%async_computation | async-start | bytes 4194304 | tf_op jit(solution)/shard_map/all_to_all | solution.py:80
  36.3 0.0 all-gather.2.cloned.1.call-start
  36.4 0.1 reshape.359
  36.4 0.1 copy.85
  36.5 0.0 copy-done.13
  36.5 0.0 copy-done.12
  36.6 0.0 copy-done.10
  36.6 0.0 copy-done.16
  36.6 0.2 fusion.51
  36.8 0.0 copy-done.6
  36.9 0.0 copy-start.7
  36.9 0.6 copy-done.7
  37.5 1.4 convolution_bitcast_fusion.3
  38.9 46.4 %all-to-all-done = bf16[1,2,16,1,128,256]{5,4,1,3,0,2:T(8,128)(2,1)} async-done(((bf16[1,2,16,1,128,256]{5,4,1,3,0,2:T(8,128)(2,1)}), bf16[1,2,16,1,128,256]{5,4,1,3,0,2:T(8,128)(2,1)}, u32[]{:S(2)}, u32[]{:S(2)}) %all-to-all-start) | async-done | bytes 2097184 | tf_op jit(solution)/shard_map/all_to_all | solution.py:80
  85.4 2.9 fusion.3
  88.2 0.0 copy-done.17
  88.3 1.1 fusion.19
  89.4 0.1 copy-done.2
  89.5 0.3 fusion.42
  89.8 0.7 copy.92
  90.5 0.0 all-gather.2.cloned.1.call-update
  90.5 0.0 all-reduce.5.cloned.1.call-start
  90.6 0.7 fusion.69
  91.3 1.4 convolution_bitcast_fusion.1
  92.7 42.5 %all-gather.2.cloned.1.call-done = bf16[1,2,32,128,256]{4,3,1,0,2:T(8,128)(2,1)} async-done(((bf16[1,2,2,128,256]{4,3,1,0,2:T(8,128)(2,1)}), bf16[1,2,32,128,256]{4,3,1,0,2:T(8,128)(2,1)}) %all-gather.2.cloned.1.call-update) | async-done | bytes 4194320 | tf_op jit(solution)/shard_map/all_gather | solution.py:57
  135.2 4.7 %convert_bitcast_fusion = bf16[1,2,12,128,256]{4,2,3,1,0:T(8,128)(2,1)S(1)} fusion(bf16[1,2,32,128,256]{4,3,1,0,2:T(8,128)(2,1)} %all-gather.2.cloned.1.call-done, s32[12]{0:T(128)S(1)} %fusion.69), kind=kOutput, calls=%fused_computation.9 | convolution fusion | flops 51118464 | bytes 5767216 | tf_op jit(solution)/shard_map/en,btnqc->bteqc/dot_general | solution.py:60
  139.9 0.6 copy.94
  140.5 0.0 copy-start.3
  140.5 0.4 fusion.25
  140.9 0.0 copy-start.8
  140.9 0.5 copy-done.3
  141.4 1.1 convolution_bitcast_fusion.4
  142.6 0.0 all-reduce.5.cloned.1.call-update
  142.6 0.5 convolution_bitcast_fusion.2
  143.1 0.8 fusion.32
  143.9 275.5 %all-reduce.5.cloned.1.call-done = (f32[512,512]{1,0:T(8,128)}, f32[512,256]{1,0:T(8,128)}) async-done(((f32[512,512]{1,0:T(8,128)}, f32[512,256]{1,0:T(8,128)}), (f32[512,512]{1,0:T(8,128)}, f32[512,256]{1,0:T(8,128)})) %all-reduce.5.cloned.1.call-update) | async-done | bytes 1572880 | tf_op jit(solution)/shard_map/psum | solution.py:104
  419.4 2.3 slice_multiply_fusion
  421.7 0.8 broadcast_multiply_fusion
  (24 shorter events, 0.3 us)
Async XLA Ops:
  7.2 6.5 %copy-start = (bf16[2,6,128,128]{3,2,1,0:T(8,128)(2,1)S(1)}, bf16[2,6,128,128]{3,2,1,0:T(8,128)(2,1)}, u32[]{:S(2)}) copy-start(bf16[2,6,128,128]{3,2,1,0:T(8,128)(2,1)} %param.13) | copy-start | bytes 1179652
  8.1 0.6 copy-start.15
  8.8 4.9 %copy-start.9 = (s32[16,12]{0,1:T(8,128)}, s32[16,12]{0,1:T(8,128)S(1)}, u32[]{:S(2)}) copy-start(s32[16,12]{0,1:T(8,128)S(1)} %copy.74) | copy-start | bytes 2308
  10.6 3.1 copy-start.11
  12.7 1.0 copy-start.1
  25.2 11.4 %copy-start.13 = (bf16[1,2,256,256]{3,2,1,0:T(8,128)(2,1)S(1)}, bf16[1,2,256,256]{3,2,1,0:T(8,128)(2,1)}, u32[]{:S(2)}) copy-start(bf16[1,2,256,256]{3,2,1,0:T(8,128)(2,1)} %param.7) | copy-start | bytes 786436
  25.2 11.4 %copy-start.12 = (s32[16,12]{0,1:T(8,128)S(1)}, s32[16,12]{0,1:T(8,128)}, u32[]{:S(2)}) copy-start(s32[16,12]{0,1:T(8,128)} %copy-done.11) | copy-start | bytes 2308
  25.2 11.4 %copy-start.10 = (s32[16,12]{0,1:T(8,128)S(1)}, s32[16,12]{0,1:T(8,128)}, u32[]{:S(2)}) copy-start(s32[16,12]{0,1:T(8,128)} %copy-done.9) | copy-start | bytes 2308
  25.2 11.5 %copy-start.16 = (s32[16,12]{0,1:T(8,128)S(1)}, s32[16,12]{0,1:T(8,128)}, u32[]{:S(2)}) copy-start(s32[16,12]{0,1:T(8,128)} %get-tuple-element.19) | copy-start | bytes 2308
  25.2 11.7 %copy-start.5 = (bf16[2,256,256]{2,1,0:T(8,128)(2,1)S(1)}, bf16[2,256,256]{2,1,0:T(8,128)(2,1)}, u32[]{:S(2)}) copy-start(bf16[2,256,256]{2,1,0:T(8,128)(2,1)} %param.10) | copy-start | bytes 786436
  25.2 11.6 %copy-start.6 = (bf16[2,256,256]{2,1,0:T(8,128)(2,1)S(1)}, bf16[2,256,256]{2,1,0:T(8,128)(2,1)}, u32[]{:S(2)}) copy-start(bf16[2,256,256]{2,1,0:T(8,128)(2,1)} %param.9) | copy-start | bytes 786436
  25.2 60.2 %all-to-all-start = ((bf16[1,2,16,1,128,256]{5,4,1,3,0,2:T(8,128)(2,1)}), bf16[1,2,16,1,128,256]{5,4,1,3,0,2:T(8,128)(2,1)}, u32[]{:S(2)}, u32[]{:S(2)}) async-start(bf16[1,2,16,1,128,256]{5,4,1,3,0,2:T(8,128)(2,1)} %copy.82), calls=%async_computation | async-start | bytes 4194304 | tf_op jit(solution)/shard_map/all_to_all | solution.py:80
  36.3 98.9 %all-gather.2.cloned.1.call-start = ((), (), s32[]{:S(2)}) async-start(), calls=%async_computation.1 | async-start | bytes 4456448 | tf_op jit(solution)/shard_map/all_gather | solution.py:57
  36.9 0.7 copy-start.7
  38.9 49.3 %copy-start.17 = (pred[12]{0:T(512)(128)(4,1)S(1)}, pred[12]{0:T(512)(128)(4,1)}, u32[]{:S(2)}) copy-start(pred[12]{0:T(512)(128)(4,1)} %get-tuple-element.6) | copy-start | bytes 40
  88.2 1.2 copy-start.2
  89.5 1.8 copy-start.14
  90.5 328.8 %all-reduce.5.cloned.1.call-start = ((), (), s32[]{:S(2)}) async-start(), calls=%async_computation.2 | async-start | bytes 3145728 | tf_op jit(solution)/shard_map/psum | solution.py:104
  140.5 1.0 copy-start.3
  140.9 1.7 copy-start.8
  419.4 2.3 copy-start.4
Sparse Core Ops, SparseCore 0:
  90.6 44.5 all-gather.1
  142.7 276.6 all-reduce.4
where the time goes:
time: 430 us; the launch traced here: 429 us
  waiting for transfers between devices  364 us (85%)
  local copies, waits for them, and re-layouts  17 us (4%)
  matrix products  15.4 us (4%)
  between operations  14.3 us (3%)
  starting transfers between devices  11.2 us (3%)
  other arithmetic  6.99 us (2%)
    psum x1, waiting for transfers between devices, per_device(): conv_total, mix_total = lax.psum((conv_sum, mix_sum), ('dp', 'region'))  275 us
    all_to_all x1, waiting for transfers between devices, per_device(): lax.all_to_all(outgoing_back, 'region', split_axis=2, concat_axis=2, tile...  46.4 us
    all_gather x1, waiting for transfers between devices, per_device(): piece = lax.all_gather(tiled, 'region', axis=2, tiled=True)  42.5 us
    all_to_all x1, starting transfers between devices, per_device(): lax.all_to_all(outgoing_back, 'region', split_axis=2, concat_axis=2, tile...  11.1 us
  transfers between devices with their start and end apart: 3, of which 3 were waited for; matrix products, arithmetic and copies ran while one was open for 1% of the time, Pallas kernels for 0%

commit v1 on v0

--- a/solution.py
+++ b/solution.py
@@ -5,6 +5,9 @@
 from jax.sharding import PartitionSpec as P
 
 CAP = 1
+wait_the_sections = lambda piece_in: jnp.concatenate(
+    lax.all_to_all(jnp.stack([piece_in for _ in range(lax.axis_size("region"))]), "region", 0, 0), 2
+)
 
 
 def per_device(inputs, cotangent, w_filter, w_gate, w_mix, neighbours, adjacency):
@@ -54,7 +57,7 @@
     gate = jax.nn.sigmoid(act[..., chans:])
     hidden = (filt * gate).astype(jnp.bfloat16)
     tiled = hidden.reshape(windows, steps, tiles_dev, 128, chans)
-    piece = lax.all_gather(tiled, "region", axis=2, tiled=True)
+    piece = wait_the_sections(tiled)
     count = piece.shape[2]
     select = (own_tiles[:, None] == jnp.arange(count)[None, :]).astype(jnp.bfloat16)
     chosen = jnp.einsum("en,btnqc->bteqc", select, piece, preferred_element_type=jnp.float32)

time: 430 us -> 505 us (1.17)
  waiting for transfers between devices: 364 us -> 414 us
  local copies, waits for them, and re-layouts: 17 us -> 38.4 us
  starting transfers between devices: 11.2 us -> 16.4 us
    all_to_all x0 -> x1, waiting for transfers between devices: none -> 91.1 us  [lax.all_to_all(jnp.stack([piece_in for _ in range(lax.axis_size('region')...]
    all_gather x1 -> x0, waiting for transfers between devices: 42.5 us -> none  [per_device(): piece = lax.all_gather(tiled, 'region', axis=2, tiled=True)]
    another operation x0 -> x3, local copies, waits for them, and re-layouts: none -> 13.2 us
    reshape x1, local copies, waits for them, and re-layouts: 0.72 us -> 8.95 us  [jnp.concatenate(lax.all_to_all(jnp.stack([piece_in for _ in range(lax.axi...]
    all_to_all x0 -> x1, starting transfers between devices: none -> 5.11 us  [lax.all_to_all(jnp.stack([piece_in for _ in range(lax.axis_size('region')...]
where the time goes in v1:
time: 505 us; the launch traced here: 504 us
  waiting for transfers between devices  414 us (82%)
  local copies, waits for them, and re-layouts  38.4 us (8%)
  starting transfers between devices  16.4 us (3%)
  between operations  14.3 us (3%)
  matrix products  13.8 us (3%)
  other arithmetic  6.99 us (1%)
    psum x1, waiting for transfers between devices, per_device(): conv_total, mix_total = lax.psum((conv_sum, mix_sum), ('dp', 'region'))  277 us
    all_to_all x1, waiting for transfers between devices, lax.all_to_all(jnp.stack([piece_in for _ in range(lax.axis_size('region')...  91.1 us
    all_to_all x1, waiting for transfers between devices, per_device(): lax.all_to_all(outgoing_back, 'region', split_axis=2, concat_axis=2, tile...  46.5 us
    all_to_all x1, starting transfers between devices, per_device(): lax.all_to_all(outgoing_back, 'region', split_axis=2, concat_axis=2, tile...  11.1 us
  transfers between devices with their start and end apart: 3, of which 3 were waited for; matrix products, arithmetic and copies ran while one was open for 1% of the time, Pallas kernels for 0%

profile of v1, /device:TPU:17, one launch (start us, length us, event | category | flops | bytes accessed | tf_op | source)
XLA Modules:
  0.0 504.2 jit_solution(12612671952381902416)
XLA Ops:
  7.2 0.0 copy-start
  7.2 0.8 copy.73
  8.0 0.1 reshape.360
  8.1 0.6 copy-done.15
  8.7 0.1 copy.74
  8.8 0.6 negate_select_fusion.4
  9.4 0.1 copy.78
  9.5 0.8 fusion.76
  10.2 0.4 convert_reduce_fusion
  10.6 0.0 copy-start.11
  10.6 0.2 select_reduce_fusion
  10.8 0.6 fusion.65
  11.4 1.4 convolution_bitcast_fusion
  12.7 0.0 copy-start.1
  12.8 0.9 copy-done.1
  13.7 0.0 copy-done.9
  13.7 0.0 copy-done.11
  13.7 0.0 copy-done
  13.7 0.6 fusion.7
  14.3 0.7 copy.80
  15.0 0.1 copy.81
  15.2 1.6 broadcast.248
  16.8 5.3 %scatter_fusion = bf16[2,16,128,256]{3,2,1,0:T(8,128)(2,1)} fusion(bf16[2,16,128,256]{3,2,1,0:T(8,128)(2,1)} %broadcast.248, s32[12]{0:T(128)} %fusion.65, bf16[12,2,128,256]{3,2,1,0:T(8,128)(2,1)S(1)} %copy.81), kind=kCustom, calls=%fused_computation | custom fusion | bytes 4718640 | tf_op jit(solution)/shard_map/scatter | solution.py:81
  22.1 3.1 copy.82
  25.2 0.0 copy-start.5
  25.2 0.0 copy-start.6
  25.2 11.1 %all-to-all-start = ((bf16[1,2,16,1,128,256]{5,4,1,3,0,2:T(8,128)(2,1)}), bf16[1,2,16,1,128,256]{5,4,1,3,0,2:T(8,128)(2,1)}, u32[]{:S(2)}, u32[]{:S(2)}) async-start(bf16[1,2,16,1,128,256]{5,4,1,3,0,2:T(8,128)(2,1)} %copy.82), calls=%async_computation | async-start | bytes 4194304 | tf_op jit(solution)/shard_map/all_to_all | solution.py:83
  36.3 0.1 reshape.365
  36.4 0.1 copy.85
  36.5 0.0 copy-done.13
  36.5 0.0 copy-done.12
  36.6 0.0 copy-done.10
  36.6 0.2 fusion.46
  36.8 0.0 copy-done.5
  36.9 0.0 copy-start.7
  36.9 0.6 copy-done.7
  37.5 1.4 convolution_bitcast_fusion.3
  38.9 46.5 %all-to-all-done = bf16[1,2,16,1,128,256]{5,4,1,3,0,2:T(8,128)(2,1)} async-done(((bf16[1,2,16,1,128,256]{5,4,1,3,0,2:T(8,128)(2,1)}), bf16[1,2,16,1,128,256]{5,4,1,3,0,2:T(8,128)(2,1)}, u32[]{:S(2)}, u32[]{:S(2)}) %all-to-all-start) | async-done | bytes 2097184 | tf_op jit(solution)/shard_map/all_to_all | solution.py:83
  85.4 2.9 fusion
  88.3 1.1 fusion.14
  89.4 0.1 copy-done.2
  89.5 0.3 fusion.37
  89.8 0.3 copy.92
  90.1 5.7 %stack.3 = bf16[16,1,2,2,128,256]{5,3,4,2,1,0:T(2,128)(2,1)} broadcast(bf16[2,2,128,256]{3,1,2,0:T(2,128)(2,1)S(1)} %copy.92), dimensions={2,3,4,5} | broadcast | bytes 4456448 | tf_op jit(solution)/shard_map/stack | solution.py:9
  95.8 5.1 %all-to-all-start.1 = ((bf16[16,1,2,2,128,256]{5,3,4,2,1,0:T(2,128)(2,1)}), bf16[16,1,2,2,128,256]{5,3,4,2,1,0:T(2,128)(2,1)}, u32[]{:S(2)}, u32[]{:S(2)}) async-start(bf16[16,1,2,2,128,256]{5,3,4,2,1,0:T(2,128)(2,1)} %stack.3), calls=%async_computation.1 | async-start | bytes 8388608 | tf_op jit(solution)/shard_map/all_to_all | solution.py:9
  100.9 0.2 all-reduce.5.cloned.1.call-start
  101.2 0.7 fusion.64
  101.9 1.5 convolution_bitcast_fusion.1
  103.4 91.1 %all-to-all-done.1 = bf16[16,1,2,2,128,256]{5,3,4,2,1,0:T(2,128)(2,1)} async-done(((bf16[16,1,2,2,128,256]{5,3,4,2,1,0:T(2,128)(2,1)}), bf16[16,1,2,2,128,256]{5,3,4,2,1,0:T(2,128)(2,1)}, u32[]{:S(2)}, u32[]{:S(2)}) %all-to-all-start.1) | async-done | bytes 4194336 | tf_op jit(solution)/shard_map/all_to_all | solution.py:9
  194.5 8.9 %copy.93 = bf16[1,2,16,2,128,256]{5,3,2,4,1,0:T(2,128)(2,1)} copy(bf16[1,2,16,2,128,256]{5,3,4,1,0,2:T(2,128)(2,1)} %bitcast.37) | data formatting | bytes 8388608 | tf_op jit(solution)/shard_map/reshape | solution.py:8
  203.5 7.2 %reshape.372 = bf16[2,32,128,256]{3,1,2,0:T(8,128)(2,1)} reshape(bf16[1,2,16,2,128,256]{5,3,2,4,1,0:T(2,128)(2,1)} %copy.93) | data formatting | bytes 8388608 | tf_op jit(solution)/shard_map/reshape.30
  210.7 2.9 convert_bitcast_fusion
  213.6 0.5 copy.94
  214.2 0.0 copy-start.3
  214.2 0.4 fusion.20
  214.6 0.0 copy-start.8
  214.6 0.5 copy-done.3
  215.1 1.1 convolution_bitcast_fusion.4
  216.3 0.0 all-reduce.5.cloned.1.call-update
  216.3 0.5 convolution_bitcast_fusion.2
  216.8 0.8 fusion.27
  217.6 276.6 %all-reduce.5.cloned.1.call-done = (f32[512,512]{1,0:T(8,128)}, f32[512,256]{1,0:T(8,128)}) async-done(((f32[512,512]{1,0:T(8,128)}, f32[512,256]{1,0:T(8,128)}), (f32[512,512]{1,0:T(8,128)}, f32[512,256]{1,0:T(8,128)})) %all-reduce.5.cloned.1.call-update) | async-done | bytes 1572880 | tf_op jit(solution)/shard_map/psum | solution.py:107
  494.2 2.3 slice_multiply_fusion
  496.5 0.8 broadcast_multiply_fusion
  (26 shorter events, 0.3 us)
Async XLA Ops:
  7.2 6.5 %copy-start = (bf16[2,6,128,128]{3,2,1,0:T(8,128)(2,1)S(1)}, bf16[2,6,128,128]{3,2,1,0:T(8,128)(2,1)}, u32[]{:S(2)}) copy-start(bf16[2,6,128,128]{3,2,1,0:T(8,128)(2,1)} %param.13) | copy-start | bytes 1179652
  8.1 0.6 copy-start.15
  8.8 4.9 copy-start.9
  10.6 3.1 copy-start.11
  12.7 1.0 copy-start.1
  25.2 11.3 %copy-start.13 = (bf16[1,2,256,256]{3,2,1,0:T(8,128)(2,1)S(1)}, bf16[1,2,256,256]{3,2,1,0:T(8,128)(2,1)}, u32[]{:S(2)}) copy-start(bf16[1,2,256,256]{3,2,1,0:T(8,128)(2,1)} %param.7) | copy-start | bytes 786436
  25.2 11.3 %copy-start.12 = (s32[16,12]{0,1:T(8,128)S(1)}, s32[16,12]{0,1:T(8,128)}, u32[]{:S(2)}) copy-start(s32[16,12]{0,1:T(8,128)} %copy-done.11) | copy-start | bytes 2308
  25.2 11.4 %copy-start.10 = (s32[16,12]{0,1:T(8,128)S(1)}, s32[16,12]{0,1:T(8,128)}, u32[]{:S(2)}) copy-start(s32[16,12]{0,1:T(8,128)} %copy-done.9) | copy-start | bytes 2308
  25.2 11.4 %copy-start.16 = (s32[16,12]{0,1:T(8,128)S(1)}, s32[16,12]{0,1:T(8,128)}, u32[]{:S(2)}) copy-start(s32[16,12]{0,1:T(8,128)} %get-tuple-element.19) | copy-start | bytes 2308
  25.2 11.6 %copy-start.5 = (bf16[2,256,256]{2,1,0:T(8,128)(2,1)S(1)}, bf16[2,256,256]{2,1,0:T(8,128)(2,1)}, u32[]{:S(2)}) copy-start(bf16[2,256,256]{2,1,0:T(8,128)(2,1)} %param.10) | copy-start | bytes 786436
  25.2 11.6 %copy-start.6 = (bf16[2,256,256]{2,1,0:T(8,128)(2,1)S(1)}, bf16[2,256,256]{2,1,0:T(8,128)(2,1)}, u32[]{:S(2)}) copy-start(bf16[2,256,256]{2,1,0:T(8,128)(2,1)} %param.9) | copy-start | bytes 786436
  25.2 60.2 %all-to-all-start = ((bf16[1,2,16,1,128,256]{5,4,1,3,0,2:T(8,128)(2,1)}), bf16[1,2,16,1,128,256]{5,4,1,3,0,2:T(8,128)(2,1)}, u32[]{:S(2)}, u32[]{:S(2)}) async-start(bf16[1,2,16,1,128,256]{5,4,1,3,0,2:T(8,128)(2,1)} %copy.82), calls=%async_computation | async-start | bytes 4194304 | tf_op jit(solution)/shard_map/all_to_all | solution.py:83
  36.9 0.7 copy-start.7
  38.9 49.4 %copy-start.17 = (pred[12]{0:T(512)(128)(4,1)S(1)}, pred[12]{0:T(512)(128)(4,1)}, u32[]{:S(2)}) copy-start(pred[12]{0:T(512)(128)(4,1)} %get-tuple-element.6) | copy-start | bytes 40
  88.3 1.2 copy-start.2
  95.8 6.0 %copy-start.14 = (bf16[1,2,256,256]{3,2,1,0:T(8,128)(2,1)S(1)}, bf16[1,2,256,256]{3,2,1,0:T(8,128)(2,1)}, u32[]{:S(2)}) copy-start(bf16[1,2,256,256]{3,2,1,0:T(8,128)(2,1)} %param.7) | copy-start | bytes 786436
  95.8 98.7 %all-to-all-start.1 = ((bf16[16,1,2,2,128,256]{5,3,4,2,1,0:T(2,128)(2,1)}), bf16[16,1,2,2,128,256]{5,3,4,2,1,0:T(2,128)(2,1)}, u32[]{:S(2)}, u32[]{:S(2)}) async-start(bf16[16,1,2,2,128,256]{5,3,4,2,1,0:T(2,128)(2,1)} %stack.3), calls=%async_computation.1 | async-start | bytes 8388608 | tf_op jit(solution)/shard_map/all_to_all | solution.py:9
  100.9 393.3 %all-reduce.5.cloned.1.call-start = ((), (), s32[]{:S(2)}) async-start(), calls=%async_computation.2 | async-start | bytes 3145728 | tf_op jit(solution)/shard_map/psum | solution.py:107
  214.2 1.0 copy-start.3
  214.6 1.7 copy-start.8
  494.2 2.3 copy-start.4
Sparse Core Ops, SparseCore 0:
  216.4 277.7 all-reduce.4
